TPU v7x, 32 devices: a whole 2x2x4 slice. The times are simulated.
32 devices in a mesh: expert: 4 (over y, x), shard: 8 (over z, core).
Axes of the slice: x: 2, y: 2, z: 4, core: 2. Of those that a mesh axis runs over, the one named last changes fastest.
Arguments:
- hidden: bfloat16 [64, 4096], P('shard'), may hold values from -6 to 6
- queries: bfloat16 [64, 32, 128], P('shard', 'expert'), may hold values from -30 to 30
- key_cache: bfloat16 [64, 512, 8, 128], P('shard', None, 'expert'), may hold values from -16 to 16
- value_cache: bfloat16 [64, 512, 8, 128], P('shard', None, 'expert'), may hold values from -6 to 6
- out_weight: bfloat16 [4096, 4096], P('expert', 'shard'), may hold values from -0.09375 to 0.09375
- norm_gain: bfloat16 [4096], replicated, may hold values from 0.099609375 to 1.8984375
- router: bfloat16 [4096, 8], replicated, may hold values from -0.09375 to 0.09375
- expert_ids: int32 [64, 2], replicated, may hold values from 0 to 7, all different within a row; in each aligned block of 64 rows (0 to 63, 64 to 127, ...) at most 32 rows name the same one
- gate_weight: bfloat16 [8, 4096, 14336], P('expert', None, 'shard'), may hold values from -0.09375 to 0.09375
- up_weight: bfloat16 [8, 4096, 14336], P('expert', None, 'shard'), may hold values from -0.09375 to 0.09375
- down_weight: bfloat16 [8, 14336, 4096], P('expert', 'shard'), may hold values from -0.046875 to 0.046875
Outputs:
- layer_out: bfloat16 [64, 4096], P('shard')
Inputs may be any that keep to these rules, and one draw needn't show every extreme that they name: `expert_ids`: each token names two different experts; over all 64 tokens no expert is named by more than 32 tokens, a bound that some block reaches.
All inputs are finite; a program needn't handle non-finite values.
Results may differ from a plain program's by a relative error of at most 0.008.
Values may be sent and summed in bfloat16 or wider, within the bound.
A program may use at most 128 MiB of HBM per device.

v0:
```python
import math
import jax
import jax.numpy as jnp
from jax import lax
from jax.sharding import PartitionSpec as P


def on_device(
    hidden,
    queries,
    key_cache,
    value_cache,
    out_weight,
    norm_gain,
    router,
    expert_ids,
    gate_weight,
    up_weight,
    down_weight,
):
    count_local, heads_local, head_size = queries.shape
    kv_local = key_cache.shape[2]
    per_kv = heads_local // kv_local
    query_blocks = queries.reshape(count_local, kv_local, per_kv, head_size)
    scores = jnp.einsum(
        "tkgd,tpkd->tkgp", query_blocks, key_cache, preferred_element_type=jnp.float32
    ) / math.sqrt(head_size)
    attn_weights = jax.nn.softmax(scores, axis=-1).astype(jnp.bfloat16)
    attended = jnp.einsum(
        "tkgp,tpkd->tkgd", attn_weights, value_cache, preferred_element_type=jnp.float32
    )
    attended = attended.astype(jnp.bfloat16).reshape(count_local, heads_local * head_size)
    all_attended = lax.all_gather(attended, "shard", axis=0, tiled=True)
    partial_cols = jnp.dot(all_attended, out_weight, preferred_element_type=jnp.float32)
    partial_heads = lax.all_to_all(partial_cols, "shard", split_axis=0, concat_axis=1, tiled=True)
    attn_out = lax.psum(partial_heads, "expert")
    stream = hidden.astype(jnp.float32) + attn_out
    scaled = stream * lax.rsqrt(jnp.mean(stream * stream, axis=-1, keepdims=True) + 1e-05)
    normed = (scaled * norm_gain.astype(jnp.float32)).astype(jnp.bfloat16)
    everyone = lax.all_gather(normed, "shard", axis=0, tiled=True)
    token_count = everyone.shape[0]
    logits = jnp.dot(everyone, router, preferred_element_type=jnp.float32)
    top_first = jnp.take_along_axis(logits, expert_ids[:, 0:1], axis=1)[:, 0]
    top_second = jnp.take_along_axis(logits, expert_ids[:, 1:2], axis=1)[:, 0]
    weight_first = 1.0 / (1.0 + jnp.exp(top_second - top_first))
    weight_second = 1.0 / (1.0 + jnp.exp(top_first - top_second))
    local_experts = gate_weight.shape[0]
    group_index = lax.axis_index("expert")
    summed = jnp.zeros((token_count, everyone.shape[1]), jnp.float32)
    for member in range(local_experts):
        expert = group_index * local_experts + member
        in_first = expert_ids[:, 0] == expert
        in_second = expert_ids[:, 1] == expert
        routed_weight = jnp.where(in_first, weight_first, 0.0) + jnp.where(
            in_second, weight_second, 0.0
        )
        gated = jnp.dot(everyone, gate_weight[member], preferred_element_type=jnp.float32)
        upward = jnp.dot(everyone, up_weight[member], preferred_element_type=jnp.float32)
        activated = (jax.nn.silu(gated) * upward).astype(jnp.bfloat16)
        expert_out = jnp.dot(activated, down_weight[member], preferred_element_type=jnp.float32)
        summed = summed + routed_weight[:, None] * expert_out
    reduced = lax.psum_scatter(summed, "shard", scatter_dimension=0, tiled=True)
    expert_mix = lax.psum(reduced, "expert")
    return (stream + expert_mix).astype(jnp.bfloat16)


def solution(mesh):
    in_specs = (
        P("shard", None),
        P("shard", "expert", None),
        P("shard", None, "expert", None),
        P("shard", None, "expert", None),
        P("expert", "shard"),
        P(),
        P(),
        P(),
        P("expert", None, "shard"),
        P("expert", None, "shard"),
        P("expert", "shard", None),
    )
    out_specs = P("shard", None)
    return jax.shard_map(
        on_device, mesh=mesh, in_specs=in_specs, out_specs=out_specs, check_vma=False
    )
```

profile of v0, /device:TPU:0, one launch (start us, length us, event | category | flops | bytes accessed | tf_op | source)
XLA Modules:
  0.0 225.8 jit_solution(6295233523832174419)
XLA Ops:
  6.5 1.6 copy-done
  8.1 1.4 fusion.46
  9.5 0.2 fusion.79
  9.7 2.0 fusion.49
  11.8 15.7 %all_gather.6 = bf16[64,1024]{1,0:T(8,128)(2,1)S(1)} all-gather(bf16[8,1024]{1,0:T(8,128)(2,1)S(1)} %reshape.37), channel_id=1, replica_groups=mesh['expert'=4,'shard'=8] {'shard'}, dimensions={0}, use_global_device_ids=true | all-gather | bytes 147456 | tf_op jit(solution)/shard_map/all_gather | solution.py:33
  27.5 2.2 convolution_bitcast_fusion
  29.7 4.6 %all-to-all-start = ((f32[8,8,512]{2,1,0:T(8,128)}), f32[8,8,512]{2,1,0:T(8,128)S(1)}, u32[]{:S(2)}, u32[]{:S(2)}) async-start(f32[8,8,512]{2,1,0:T(8,128)} %convolution_bitcast_fusion), calls=%async_computation | async-start | bytes 262144 | tf_op jit(solution)/shard_map/all_to_all | solution.py:35
  34.3 0.0 all-reduce.3.cloned.1.call-start
  34.3 0.7 convert_element_type.27
  35.0 0.8 fusion.78
  35.8 5.2 %all-to-all-done = f32[8,8,512]{2,1,0:T(8,128)S(1)} async-done(((f32[8,8,512]{2,1,0:T(8,128)}), f32[8,8,512]{2,1,0:T(8,128)S(1)}, u32[]{:S(2)}, u32[]{:S(2)}) %all-to-all-start) | async-done | bytes 131104 | tf_op jit(solution)/shard_map/all_to_all | solution.py:35
  41.0 0.6 copy-done.4
  41.7 0.0 all-reduce.3.cloned.1.call-update
  41.7 0.0 reduce-scatter.2.cloned.1.call-start
  41.8 41.4 %all-reduce.3.cloned.1.call-done = f32[8,4096]{1,0:T(8,128)} async-done(((f32[8,4096]{1,0:T(8,128)}), f32[8,4096]{1,0:T(8,128)}) %all-reduce.3.cloned.1.call-update) | async-done | bytes 131088 | tf_op jit(solution)/shard_map/psum | solution.py:36
  83.2 1.1 multiply_reduce_fusion
  84.2 1.0 multiply_convert_fusion
  85.2 14.7 %all_gather.7 = bf16[64,4096]{1,0:T(8,128)(2,1)S(1)} all-gather(bf16[8,4096]{1,0:T(8,128)(2,1)S(1)} %multiply_convert_fusion), channel_id=1, replica_groups=mesh['expert'=4,'shard'=8] {'shard'}, dimensions={0}, use_global_device_ids=true | all-gather | bytes 589824 | tf_op jit(solution)/shard_map/all_gather | solution.py:40
  100.0 6.5 %fusion.5 = f32[64,1792]{1,0:T(8,128)S(1)} fusion(bf16[64,4096]{1,0:T(8,128)(2,1)S(1)} %all_gather.7, bf16[2,4096,1792]{2,1,0:T(8,128)(2,1)} %param.21), kind=kOutput, calls=%fused_computation.7 | convolution fusion | flops 939524096 | bytes 15663104 | tf_op jit(solution)/shard_map/dot_general | solution.py:57
  106.4 6.4 %fusion.11 = f32[64,1792]{1,0:T(8,128)S(1)} fusion(bf16[64,4096]{1,0:T(8,128)(2,1)S(1)} %all_gather.7, bf16[2,4096,1792]{2,1,0:T(8,128)(2,1)} %param.21), kind=kOutput, calls=%fused_computation.13 | convolution fusion | flops 939524096 | bytes 15663104 | tf_op jit(solution)/shard_map/dot_general | solution.py:57
  112.9 0.2 fusion.80
  113.2 0.7 gather_fusion
  113.9 0.7 gather_fusion.1
  114.7 13.1 %fusion.25 = f32[64,4096]{1,0:T(8,128)} fusion(bf16[2,1792,4096]{2,1,0:T(8,128)(2,1)} %param.23, bf16[64,4096]{1,0:T(8,128)(2,1)S(1)} %all_gather.7, bf16[2,4096,1792]{2,1,0:T(8,128)(2,1)} %param.22, f32[64]{0:T(128)S(1)} %fusion.73, f32[64,1792]{1,0:T(8,128)S(1)} %fusion.5), kind=kOutput, calls=%fused_computation.23 | convolution fusion | flops 1879998464 | bytes 31392000 | tf_op jit(solution)/shard_map/dot_general | solution.py:60
  127.8 13.6 %fusion.22 = f32[64,4096]{1,0:T(8,128)} fusion(f32[64,4096]{1,0:T(8,128)} %fusion.25, bf16[2,1792,4096]{2,1,0:T(8,128)(2,1)} %param.23, bf16[64,4096]{1,0:T(8,128)(2,1)S(1)} %all_gather.7, bf16[2,4096,1792]{2,1,0:T(8,128)(2,1)} %param.22, f32[64]{0:T(128)S(1)} %get-tuple-element.6, f32[64,1792]{1,0:T(8,128)S(1)} %fusion.11), kind=kOutput, calls=%fused_computation.22 | convolution fusion | flops 1880260608 | bytes 32440576 | tf_op jit(solution)/shard_map/dot_general | solution.py:60
  141.4 0.0 reduce-scatter.2.cloned.1.call-update
  141.5 0.0 all-reduce.5.cloned.1.call-start
  141.5 32.9 %reduce-scatter.2.cloned.1.call-done = f32[8,4096]{1,0:T(8,128)} async-done(((f32[64,4096]{1,0:T(8,128)}), f32[8,4096]{1,0:T(8,128)}) %reduce-scatter.2.cloned.1.call-update) | async-done | bytes 131088 | tf_op jit(solution)/shard_map/reduce_scatter | solution.py:62
  174.4 0.0 all-reduce.5.cloned.1.call-update
  174.4 43.3 %all-reduce.5.cloned.1.call-done = f32[8,4096]{1,0:T(8,128)} async-done(((f32[8,4096]{1,0:T(8,128)}), f32[8,4096]{1,0:T(8,128)}) %all-reduce.5.cloned.1.call-update) | async-done | bytes 131088 | tf_op jit(solution)/shard_map/psum | solution.py:63
  217.7 1.6 add_convert_fusion
  219.2 0.0 copy-done.1
  (19 shorter events, 0.1 us)
Async XLA Ops:
  6.5 1.6 copy-start
  29.7 11.3 %all-to-all-start = ((f32[8,8,512]{2,1,0:T(8,128)}), f32[8,8,512]{2,1,0:T(8,128)S(1)}, u32[]{:S(2)}, u32[]{:S(2)}) async-start(f32[8,8,512]{2,1,0:T(8,128)} %convolution_bitcast_fusion), calls=%async_computation | async-start | bytes 262144 | tf_op jit(solution)/shard_map/all_to_all | solution.py:35
  34.3 48.9 %all-reduce.3.cloned.1.call-start = ((), (), s32[]{:S(2)}) async-start(), calls=%async_computation.2 | async-start | bytes 262144 | tf_op jit(solution)/shard_map/psum | solution.py:36
  41.0 0.6 copy-start.4
  41.7 132.7 %reduce-scatter.2.cloned.1.call-start = ((), (), s32[]{:S(2)}) async-start(), calls=%async_computation.3 | async-start | bytes 1179648 | tf_op jit(solution)/shard_map/reduce_scatter | solution.py:62
  100.0 12.9 %copy-start.5 = (bf16[4096,8]{0,1:T(8,128)(2,1)S(1)}, bf16[4096,8]{0,1:T(8,128)(2,1)}, u32[]{:S(2)}) copy-start(bf16[4096,8]{0,1:T(8,128)(2,1)} %param.19) | copy-start | bytes 196612
  100.0 14.7 %copy-start.6 = (s32[64,2]{0,1:T(2,128)S(1)}, s32[64,2]{0,1:T(2,128)}, u32[]{:S(2)}) copy-start(s32[64,2]{0,1:T(2,128)} %param.20) | copy-start | bytes 1540
  127.8 91.4 %copy-start.1 = (bf16[8,512,2,128]{3,2,1,0:T(2,128)(2,1)S(1)}, bf16[8,512,2,128]{3,2,1,0:T(2,128)(2,1)}, u32[]{:S(2)}) copy-start(bf16[8,512,2,128]{3,2,1,0:T(2,128)(2,1)} %param.15) | copy-start | bytes 6291460
  127.8 89.9 %copy-start.2 = (f32[8,4096]{1,0:T(8,128)S(1)}, f32[8,4096]{1,0:T(8,128)}, u32[]{:S(2)}) copy-start(f32[8,4096]{1,0:T(8,128)} %all-reduce.3.cloned.1.call-done) | copy-start | bytes 393220
  127.8 89.9 %copy-start.3 = (bf16[8,4096]{1,0:T(8,128)(2,1)S(1)}, bf16[8,4096]{1,0:T(8,128)(2,1)}, u32[]{:S(2)}) copy-start(bf16[8,4096]{1,0:T(8,128)(2,1)} %param.13) | copy-start | bytes 196612
  141.5 76.2 %all-reduce.5.cloned.1.call-start = ((), (), s32[]{:S(2)}) async-start(), calls=%async_computation.4 | async-start | bytes 262144 | tf_op jit(solution)/shard_map/psum | solution.py:63
Sparse Core Ops, SparseCore 0:
  41.8 41.2 all-reduce.2
  141.6 32.7 reduce-scatter.1
  177.3 40.3 all-reduce.4
where the time goes:
time: 226 us
  waiting for transfers between devices  123 us (54%)
  matrix products  45.5 us (20%)
  blocking collectives  30.5 us (13%)
  between operations  13.2 us (6%)
  other arithmetic  5.35 us (2%)
  starting transfers between devices  4.72 us (2%)
  local copies, waits for them, and re-layouts  3.76 us (2%)
    psum x1, waiting for transfers between devices, on_device(): expert_mix = lax.psum(reduced, 'expert')  43.3 us
    psum x1, waiting for transfers between devices, on_device(): attn_out = lax.psum(partial_heads, 'expert')  41.4 us
    reduce_scatter x1, waiting for transfers between devices, on_device(): reduced = lax.psum_scatter(summed, 'shard', scatter_dimension=0, tiled=True)  32.9 us
    dot_general x2, matrix products, on_device(): jnp.dot(activated, down_weight[member], preferred_element_type=jnp.float32)  26.7 us
    all_gather x1, blocking collectives, on_device(): all_attended = lax.all_gather(attended, 'shard', axis=0, tiled=True)  15.7 us
    all_gather x1, blocking collectives, on_device(): everyone = lax.all_gather(normed, 'shard', axis=0, tiled=True)  14.7 us
    dot_general x2, matrix products, on_device(): jnp.dot(everyone, gate_weight[member], preferred_element_type=jnp.float32)  12.9 us
    all_to_all x1, waiting for transfers between devices, on_device(): lax.all_to_all(partial_cols, 'shard', split_axis=0, concat_axis=1, tiled=...  5.22 us
  transfers between devices with their start and end apart: 4, of which 4 were waited for; matrix products, arithmetic and copies ran while one was open for 1% of the time, Pallas kernels for 0%

commit v1 on v0

--- a/solution.py
+++ b/solution.py
@@ -18,6 +18,21 @@
     up_weight,
     down_weight,
 ):
+
+    def _state_works(buf):
+        slots = []
+        full_n = lax.axis_size("shard")
+        for kk in [*range(1, full_n)]:
+            slots.append((kk - 1, kk))
+        f_next = slots + [(full_n - 1, 0)]
+        x_new = buf
+        copies = [x_new]
+        for _ in [*range(full_n - 1)]:
+            x_new = lax.ppermute(x_new, "shard", f_next)
+            copies += [x_new]
+        fresh = jnp.concatenate([*reversed(copies)], 0)
+        return jnp.roll(fresh, (lax.axis_index("shard") + 1) * x_new.shape[0], axis=0)
+
     count_local, heads_local, head_size = queries.shape
     kv_local = key_cache.shape[2]
     per_kv = heads_local // kv_local
@@ -30,7 +45,7 @@
         "tkgp,tpkd->tkgd", attn_weights, value_cache, preferred_element_type=jnp.float32
     )
     attended = attended.astype(jnp.bfloat16).reshape(count_local, heads_local * head_size)
-    all_attended = lax.all_gather(attended, "shard", axis=0, tiled=True)
+    all_attended = _state_works(attended)
     partial_cols = jnp.dot(all_attended, out_weight, preferred_element_type=jnp.float32)
     partial_heads = lax.all_to_all(partial_cols, "shard", split_axis=0, concat_axis=1, tiled=True)
     attn_out = lax.psum(partial_heads, "expert")

time: 226 us -> 246 us (1.088)
  waiting for transfers between devices: 123 us -> 158 us
  blocking collectives: 30.5 us -> 14.7 us
    ppermute x0 -> x7, waiting for transfers between devices: none -> 34.5 us  [_state_works(): x_new = lax.ppermute(x_new, 'shard', f_next)]
    all_gather x1 -> x0, blocking collectives: 15.7 us -> none  [on_device(): all_attended = lax.all_gather(attended, 'shard', axis=0, tiled=True)]
  transfers between devices with their start and end apart: 4 -> 11, of which waited for: 4 -> 11; matrix products, arithmetic and copies ran while one was open for 1% -> 1% of each run, Pallas kernels for 0% -> 0%
where the time goes in v1:
time: 246 us; the launch traced here: 245 us
  waiting for transfers between devices  158 us (64%)
  matrix products  45.4 us (18%)
  blocking collectives  14.7 us (6%)
  between operations  13.3 us (5%)
  other arithmetic  5.35 us (2%)
  starting transfers between devices  4.06 us (2%)
  local copies, waits for them, and re-layouts  3.81 us (2%)
    psum x1, waiting for transfers between devices, on_device(): expert_mix = lax.psum(reduced, 'expert')  43.4 us
    psum x1, waiting for transfers between devices, on_device(): attn_out = lax.psum(partial_heads, 'expert')  41.9 us
    ppermute x7, waiting for transfers between devices, _state_works(): x_new = lax.ppermute(x_new, 'shard', f_next)  34.5 us
    reduce_scatter x1, waiting for transfers between devices, on_device(): reduced = lax.psum_scatter(summed, 'shard', scatter_dimension=0, tiled=True)  32.9 us
    dot_general x2, matrix products, on_device(): jnp.dot(activated, down_weight[member], preferred_element_type=jnp.float32)  26.7 us
    all_gather x1, blocking collectives, on_device(): everyone = lax.all_gather(normed, 'shard', axis=0, tiled=True)  14.7 us
    dot_general x2, matrix products, on_device(): jnp.dot(everyone, gate_weight[member], preferred_element_type=jnp.float32)  12.9 us
    all_to_all x1, waiting for transfers between devices, on_device(): lax.all_to_all(partial_cols, 'shard', split_axis=0, concat_axis=1, tiled=...  5.86 us
  transfers between devices with their start and end apart: 11, of which 11 were waited for; matrix products, arithmetic and copies ran while one was open for 1% of the time, Pallas kernels for 0%

profile of v1, /device:TPU:0, one launch (start us, length us, event | category | flops | bytes accessed | tf_op | source)
XLA Modules:
  0.0 245.2 jit_solution(613235889628952572)
XLA Ops:
  6.5 1.6 copy-done
  8.1 1.4 fusion.46
  9.5 0.2 fusion.81
  9.7 2.0 fusion.49
  11.8 0.5 collective-permute-start
  12.3 5.4 %collective-permute-done = bf16[8,1024]{1,0:T(8,128)(2,1)S(1)} collective-permute-done((bf16[8,1024]{1,0:T(8,128)(2,1)S(1)}, bf16[8,1024]{1,0:T(8,128)(2,1)S(1)}, u32[]{:S(2)}, u32[]{:S(2)}) %collective-permute-start) | collective-permute-done | bytes 16416 | tf_op jit(solution)/shard_map/ppermute | solution.py:31
  17.8 5.0 %collective-permute-done.1 = bf16[8,1024]{1,0:T(8,128)(2,1)S(1)} collective-permute-done((bf16[8,1024]{1,0:T(8,128)(2,1)S(1)}, bf16[8,1024]{1,0:T(8,128)(2,1)S(1)}, u32[]{:S(2)}, u32[]{:S(2)}) %collective-permute-start.1) | collective-permute-done | bytes 16416 | tf_op jit(solution)/shard_map/ppermute | solution.py:31
  22.7 5.0 %collective-permute-done.2 = bf16[8,1024]{1,0:T(8,128)(2,1)S(1)} collective-permute-done((bf16[8,1024]{1,0:T(8,128)(2,1)S(1)}, bf16[8,1024]{1,0:T(8,128)(2,1)S(1)}, u32[]{:S(2)}, u32[]{:S(2)}) %collective-permute-start.2) | collective-permute-done | bytes 16416 | tf_op jit(solution)/shard_map/ppermute | solution.py:31
  27.7 5.0 %collective-permute-done.3 = bf16[8,1024]{1,0:T(8,128)(2,1)S(1)} collective-permute-done((bf16[8,1024]{1,0:T(8,128)(2,1)S(1)}, bf16[8,1024]{1,0:T(8,128)(2,1)S(1)}, u32[]{:S(2)}, u32[]{:S(2)}) %collective-permute-start.3) | collective-permute-done | bytes 16416 | tf_op jit(solution)/shard_map/ppermute | solution.py:31
  32.7 5.0 %collective-permute-done.4 = bf16[8,1024]{1,0:T(8,128)(2,1)S(1)} collective-permute-done((bf16[8,1024]{1,0:T(8,128)(2,1)S(1)}, bf16[8,1024]{1,0:T(8,128)(2,1)S(1)}, u32[]{:S(2)}, u32[]{:S(2)}) %collective-permute-start.4) | collective-permute-done | bytes 16416 | tf_op jit(solution)/shard_map/ppermute | solution.py:31
  37.6 5.0 %collective-permute-done.5 = bf16[8,1024]{1,0:T(8,128)(2,1)S(1)} collective-permute-done((bf16[8,1024]{1,0:T(8,128)(2,1)S(1)}, bf16[8,1024]{1,0:T(8,128)(2,1)S(1)}, u32[]{:S(2)}, u32[]{:S(2)}) %collective-permute-start.5) | collective-permute-done | bytes 16416 | tf_op jit(solution)/shard_map/ppermute | solution.py:31
  42.6 0.7 convert_element_type.27
  43.3 4.3 %collective-permute-done.6 = bf16[8,1024]{1,0:T(8,128)(2,1)S(1)} collective-permute-done((bf16[8,1024]{1,0:T(8,128)(2,1)S(1)}, bf16[8,1024]{1,0:T(8,128)(2,1)S(1)}, u32[]{:S(2)}, u32[]{:S(2)}) %collective-permute-start.6) | collective-permute-done | bytes 16416 | tf_op jit(solution)/shard_map/ppermute | solution.py:31
  47.7 2.2 convolution_bitcast_fusion
  49.9 3.4 %all-to-all-start = ((f32[8,8,512]{2,1,0:T(8,128)}), f32[8,8,512]{2,1,0:T(8,128)S(1)}, u32[]{:S(2)}, u32[]{:S(2)}) async-start(f32[8,8,512]{2,1,0:T(8,128)} %convolution_bitcast_fusion), calls=%async_computation | async-start | bytes 262144 | tf_op jit(solution)/shard_map/all_to_all | solution.py:50
  53.3 0.8 fusion.80
  54.1 5.9 %all-to-all-done = f32[8,8,512]{2,1,0:T(8,128)S(1)} async-done(((f32[8,8,512]{2,1,0:T(8,128)}), f32[8,8,512]{2,1,0:T(8,128)S(1)}, u32[]{:S(2)}, u32[]{:S(2)}) %all-to-all-start) | async-done | bytes 131104 | tf_op jit(solution)/shard_map/all_to_all | solution.py:50
  60.0 0.6 copy-done.4
  60.7 41.9 %all-reduce.3.cloned.1.call-done = f32[8,4096]{1,0:T(8,128)} async-done(((f32[8,4096]{1,0:T(8,128)}), f32[8,4096]{1,0:T(8,128)}) %all-reduce.3.cloned.1.call-update) | async-done | bytes 131088 | tf_op jit(solution)/shard_map/psum | solution.py:51
  102.5 1.1 multiply_reduce_fusion
  103.6 1.0 multiply_convert_fusion
  104.6 14.7 %all_gather.3 = bf16[64,4096]{1,0:T(8,128)(2,1)S(1)} all-gather(bf16[8,4096]{1,0:T(8,128)(2,1)S(1)} %multiply_convert_fusion), channel_id=1, replica_groups=mesh['expert'=4,'shard'=8] {'shard'}, dimensions={0}, use_global_device_ids=true | all-gather | bytes 589824 | tf_op jit(solution)/shard_map/all_gather | solution.py:55
  119.3 6.5 %fusion.5 = f32[64,1792]{1,0:T(8,128)S(1)} fusion(bf16[64,4096]{1,0:T(8,128)(2,1)S(1)} %all_gather.3, bf16[2,4096,1792]{2,1,0:T(8,128)(2,1)} %param.21), kind=kOutput, calls=%fused_computation.7 | convolution fusion | flops 939524096 | bytes 15663104 | tf_op jit(solution)/shard_map/dot_general | solution.py:72
  125.8 6.4 %fusion.11 = f32[64,1792]{1,0:T(8,128)S(1)} fusion(bf16[64,4096]{1,0:T(8,128)(2,1)S(1)} %all_gather.3, bf16[2,4096,1792]{2,1,0:T(8,128)(2,1)} %param.21), kind=kOutput, calls=%fused_computation.13 | convolution fusion | flops 939524096 | bytes 15663104 | tf_op jit(solution)/shard_map/dot_general | solution.py:72
  132.3 0.2 fusion.82
  132.5 0.7 gather_fusion
  133.3 0.7 gather_fusion.1
  134.1 13.1 %fusion.25 = f32[64,4096]{1,0:T(8,128)} fusion(bf16[2,1792,4096]{2,1,0:T(8,128)(2,1)} %param.23, bf16[64,4096]{1,0:T(8,128)(2,1)S(1)} %all_gather.3, bf16[2,4096,1792]{2,1,0:T(8,128)(2,1)} %param.22, f32[64]{0:T(128)S(1)} %fusion.74, f32[64,1792]{1,0:T(8,128)S(1)} %fusion.5), kind=kOutput, calls=%fused_computation.23 | convolution fusion | flops 1879998464 | bytes 31392000 | tf_op jit(solution)/shard_map/dot_general | solution.py:75
  147.2 13.6 %fusion.22 = f32[64,4096]{1,0:T(8,128)} fusion(f32[64,4096]{1,0:T(8,128)} %fusion.25, bf16[2,1792,4096]{2,1,0:T(8,128)(2,1)} %param.23, bf16[64,4096]{1,0:T(8,128)(2,1)S(1)} %all_gather.3, bf16[2,4096,1792]{2,1,0:T(8,128)(2,1)} %param.22, f32[64]{0:T(128)S(1)} %get-tuple-element.6, f32[64,1792]{1,0:T(8,128)S(1)} %fusion.11), kind=kOutput, calls=%fused_computation.22 | convolution fusion | flops 1880260608 | bytes 32440576 | tf_op jit(solution)/shard_map/dot_general | solution.py:75
  160.9 32.9 %reduce-scatter.2.cloned.1.call-done = f32[8,4096]{1,0:T(8,128)} async-done(((f32[64,4096]{1,0:T(8,128)}), f32[8,4096]{1,0:T(8,128)}) %reduce-scatter.2.cloned.1.call-update) | async-done | bytes 131088 | tf_op jit(solution)/shard_map/reduce_scatter | solution.py:77
  193.8 43.4 %all-reduce.5.cloned.1.call-done = f32[8,4096]{1,0:T(8,128)} async-done(((f32[8,4096]{1,0:T(8,128)}), f32[8,4096]{1,0:T(8,128)}) %all-reduce.5.cloned.1.call-update) | async-done | bytes 131088 | tf_op jit(solution)/shard_map/psum | solution.py:78
  237.1 1.6 add_convert_fusion
  (48 shorter events, 0.4 us)
Async XLA Ops:
  6.5 1.6 copy-start
  11.8 6.0 %collective-permute-start = (bf16[8,1024]{1,0:T(8,128)(2,1)S(1)}, bf16[8,1024]{1,0:T(8,128)(2,1)S(1)}, u32[]{:S(2)}, u32[]{:S(2)}) collective-permute-start(bf16[8,1024]{1,0:T(8,128)(2,1)S(1)} %reshape.37), channel_id=1, source_target_pairs={{0,1},{1,2},{2,3},{3,4},{4,5},{5,6},{6,7},{7,0},{8,9},{9,10},{10,1... | collective-permute-start | bytes 49160 | tf_op jit(solution)/shard_map/ppermute | solution.py:31
  17.8 5.0 %collective-permute-start.1 = (bf16[8,1024]{1,0:T(8,128)(2,1)S(1)}, bf16[8,1024]{1,0:T(8,128)(2,1)S(1)}, u32[]{:S(2)}, u32[]{:S(2)}) collective-permute-start(bf16[8,1024]{1,0:T(8,128)(2,1)S(1)} %collective-permute-done), channel_id=1, source_target_pairs={{0,1},{1,2},{2,3},{3,4},{4,5},{5,6},{6,7},{7,0},{8,9},{9,10},{10,1... | collective-permute-start | bytes 49160 | tf_op jit(solution)/shard_map/ppermute | solution.py:31
  22.7 5.0 %collective-permute-start.2 = (bf16[8,1024]{1,0:T(8,128)(2,1)S(1)}, bf16[8,1024]{1,0:T(8,128)(2,1)S(1)}, u32[]{:S(2)}, u32[]{:S(2)}) collective-permute-start(bf16[8,1024]{1,0:T(8,128)(2,1)S(1)} %collective-permute-done.1), channel_id=1, source_target_pairs={{0,1},{1,2},{2,3},{3,4},{4,5},{5,6},{6,7},{7,0},{8,9},{9,10},{10,1... | collective-permute-start | bytes 49160 | tf_op jit(solution)/shard_map/ppermute | solution.py:31
  27.7 5.0 %collective-permute-start.3 = (bf16[8,1024]{1,0:T(8,128)(2,1)S(1)}, bf16[8,1024]{1,0:T(8,128)(2,1)S(1)}, u32[]{:S(2)}, u32[]{:S(2)}) collective-permute-start(bf16[8,1024]{1,0:T(8,128)(2,1)S(1)} %collective-permute-done.2), channel_id=1, source_target_pairs={{0,1},{1,2},{2,3},{3,4},{4,5},{5,6},{6,7},{7,0},{8,9},{9,10},{10,1... | collective-permute-start | bytes 49160 | tf_op jit(solution)/shard_map/ppermute | solution.py:31
  32.7 5.0 %collective-permute-start.4 = (bf16[8,1024]{1,0:T(8,128)(2,1)S(1)}, bf16[8,1024]{1,0:T(8,128)(2,1)S(1)}, u32[]{:S(2)}, u32[]{:S(2)}) collective-permute-start(bf16[8,1024]{1,0:T(8,128)(2,1)S(1)} %collective-permute-done.3), channel_id=1, source_target_pairs={{0,1},{1,2},{2,3},{3,4},{4,5},{5,6},{6,7},{7,0},{8,9},{9,10},{10,1... | collective-permute-start | bytes 49160 | tf_op jit(solution)/shard_map/ppermute | solution.py:31
  37.6 5.0 %collective-permute-start.5 = (bf16[8,1024]{1,0:T(8,128)(2,1)S(1)}, bf16[8,1024]{1,0:T(8,128)(2,1)S(1)}, u32[]{:S(2)}, u32[]{:S(2)}) collective-permute-start(bf16[8,1024]{1,0:T(8,128)(2,1)S(1)} %collective-permute-done.4), channel_id=1, source_target_pairs={{0,1},{1,2},{2,3},{3,4},{4,5},{5,6},{6,7},{7,0},{8,9},{9,10},{10,1... | collective-permute-start | bytes 49160 | tf_op jit(solution)/shard_map/ppermute | solution.py:31
  42.6 5.0 %collective-permute-start.6 = (bf16[8,1024]{1,0:T(8,128)(2,1)S(1)}, bf16[8,1024]{1,0:T(8,128)(2,1)S(1)}, u32[]{:S(2)}, u32[]{:S(2)}) collective-permute-start(bf16[8,1024]{1,0:T(8,128)(2,1)S(1)} %collective-permute-done.5), channel_id=1, source_target_pairs={{0,1},{1,2},{2,3},{3,4},{4,5},{5,6},{6,7},{7,0},{8,9},{9,10},{10,1... | collective-permute-start | bytes 49160 | tf_op jit(solution)/shard_map/ppermute | solution.py:31
  49.9 10.1 %all-to-all-start = ((f32[8,8,512]{2,1,0:T(8,128)}), f32[8,8,512]{2,1,0:T(8,128)S(1)}, u32[]{:S(2)}, u32[]{:S(2)}) async-start(f32[8,8,512]{2,1,0:T(8,128)} %convolution_bitcast_fusion), calls=%async_computation | async-start | bytes 262144 | tf_op jit(solution)/shard_map/all_to_all | solution.py:50
  53.3 49.3 %all-reduce.3.cloned.1.call-start = ((), (), s32[]{:S(2)}) async-start(), calls=%async_computation.2 | async-start | bytes 262144 | tf_op jit(solution)/shard_map/psum | solution.py:51
  60.0 0.6 copy-start.4
  60.6 133.1 %reduce-scatter.2.cloned.1.call-start = ((), (), s32[]{:S(2)}) async-start(), calls=%async_computation.3 | async-start | bytes 1179648 | tf_op jit(solution)/shard_map/reduce_scatter | solution.py:77
  119.3 12.9 %copy-start.5 = (bf16[4096,8]{0,1:T(8,128)(2,1)S(1)}, bf16[4096,8]{0,1:T(8,128)(2,1)}, u32[]{:S(2)}) copy-start(bf16[4096,8]{0,1:T(8,128)(2,1)} %param.19) | copy-start | bytes 196612
  119.3 14.7 %copy-start.6 = (s32[64,2]{0,1:T(2,128)S(1)}, s32[64,2]{0,1:T(2,128)}, u32[]{:S(2)}) copy-start(s32[64,2]{0,1:T(2,128)} %param.20) | copy-start | bytes 1540
  147.2 91.5 %copy-start.1 = (bf16[8,512,2,128]{3,2,1,0:T(2,128)(2,1)S(1)}, bf16[8,512,2,128]{3,2,1,0:T(2,128)(2,1)}, u32[]{:S(2)}) copy-start(bf16[8,512,2,128]{3,2,1,0:T(2,128)(2,1)} %param.15) | copy-start | bytes 6291460
  147.2 89.9 %copy-start.2 = (f32[8,4096]{1,0:T(8,128)S(1)}, f32[8,4096]{1,0:T(8,128)}, u32[]{:S(2)}) copy-start(f32[8,4096]{1,0:T(8,128)} %all-reduce.3.cloned.1.call-done) | copy-start | bytes 393220
  147.2 89.9 %copy-start.3 = (bf16[8,4096]{1,0:T(8,128)(2,1)S(1)}, bf16[8,4096]{1,0:T(8,128)(2,1)}, u32[]{:S(2)}) copy-start(bf16[8,4096]{1,0:T(8,128)(2,1)} %param.13) | copy-start | bytes 196612
  160.8 76.3 %all-reduce.5.cloned.1.call-start = ((), (), s32[]{:S(2)}) async-start(), calls=%async_computation.4 | async-start | bytes 262144 | tf_op jit(solution)/shard_map/psum | solution.py:78
Sparse Core Ops, SparseCore 0:
  60.7 41.7 all-reduce.2
  160.9 32.7 reduce-scatter.1
  196.6 40.4 all-reduce.4
